TPU v7x, 32 devices: a whole 2x2x4 slice. The times are simulated.
32 devices in a mesh: section: 2 (over x), dp: 4 (over z), mp: 4 (over y, core).
Axes of the slice: x: 2, y: 2, z: 4, core: 2. Of those that a mesh axis runs over, the one named last changes fastest.
Arguments:
- hidden: bfloat16 [2, 512, 4096], P('section', 'dp'), may hold values from -9 to 9
- norm_gain: float32 [2, 4096], P('section'), may hold values from 0.5 to 1.5
- kv_weight: bfloat16 [2, 4096, 2048], P('section', None, 'mp'), may hold values from -1 to 1
- attn_flat: bfloat16 [2, 4, 8388608], P('section', 'mp', 'dp'), may hold values from -1 to 1
- final_gain: float32 [4096], replicated, may hold values from 0.5 to 1.5
- reward_head: float32 [4096], replicated, may hold values from -0.09375 to 0.09375
- segment_ids: int32 [2, 4], P('section'), may hold values from 0 to 2, never falling along the last dimension, each value on 1 to 2 neighbouring positions
- ranks: int32 [2], replicated, may hold values from 0 to 999
Outputs:
- next_hidden: bfloat16 [2, 512, 4096], P('section', 'dp')
- rewards: float32 [2], replicated
- pair_loss: float32 [2, 2], replicated
Inputs may be any that keep to these rules, and one draw needn't show every extreme that they name: `segment_ids`: each row's segment numbers never fall, every number of 0 to 2 is present, each on 1 to 2 blocks, one on exactly 2.
All inputs are finite; a program needn't handle non-finite values.
Results may differ from a plain program's by a relative error of at most 0.035.
Values may be sent and summed in bfloat16 or wider, within the bound.
A program may use at most 128 MiB of HBM per device.

v0:
```python
import jax
import jax.numpy as jnp
from jax import lax
from jax.sharding import PartitionSpec as P

HD = 128
QH = 32
KVH = 8


EPS = 1e-05


def passed_along(block, axis, distance):
    devices = range(lax.axis_size(axis))
    route = [(i - distance, i) for i in devices if i - distance in devices]
    return lax.ppermute(block, axis, route)


def shards(hidden, norm_gain, kv_weight, attn_flat, final_gain, reward_head, segment_ids, ranks):
    state = hidden[0]
    tokens = state.shape[0]
    width = state.shape[1]
    seg_row = segment_ids[0]
    blocks = lax.axis_size("dp")
    block = lax.axis_index("dp")
    phases = lax.axis_size("section")
    phase_now = lax.axis_index("section")
    responses = ranks.shape[0]
    state_wide = state.astype(jnp.float32)
    normed = (
        state_wide
        * lax.rsqrt(jnp.mean(state_wide * state_wide, -1, keepdims=True) + EPS)
        * norm_gain[0]
    ).astype(jnp.bfloat16)
    keyval = jnp.dot(normed, kv_weight[0], preferred_element_type=jnp.float32).astype(jnp.bfloat16)
    kv_local = keyval.shape[1] // (2 * HD)
    group = QH // KVH
    q_width = kv_local * group * HD
    flat = lax.all_gather(attn_flat[0, 0], "dp", axis=0, tiled=True)
    w_query = flat[: width * q_width].reshape(width, q_width)
    w_out = flat[width * q_width : 2 * width * q_width].reshape(q_width, width)
    query = jnp.dot(normed, w_query, preferred_element_type=jnp.float32).astype(jnp.bfloat16)
    query = query.reshape(tokens, kv_local, group, HD)
    block_ids = jnp.arange(blocks, dtype=jnp.int32)
    own_seg = jnp.sum(jnp.where(block_ids == block, seg_row, 0))
    query_pos = block * tokens + jnp.arange(tokens, dtype=jnp.int32)
    piece = lax.all_gather(keyval, "dp", axis=0, tiled=True)
    peak = jnp.full((kv_local, group, tokens), -1e30, jnp.float32)
    count = piece.shape[0]
    key_pos = jnp.arange(count, dtype=jnp.int32)
    key_block = key_pos // tokens
    key_seg = jnp.sum(jnp.where(key_block[:, None] == block_ids[None, :], seg_row[None, :], 0), 1)
    parts = piece.reshape(count, kv_local, 2, HD)
    keys = parts[:, :, 0]
    values = parts[:, :, 1]
    earlier = (key_block < block) & (key_block >= 0) & ((key_seg == 0) | (key_seg == own_seg))
    same = (key_block == block)[None, :] & (key_pos[None, :] <= query_pos[:, None])
    visible = earlier[None, :] | same
    scores = jnp.einsum("tjgd,cjd->jgtc", query, keys, preferred_element_type=jnp.float32) * HD ** (
        -0.5
    )
    scores = jnp.where(visible[None, None], scores, -1e30)
    new_peak = jnp.maximum(peak, jnp.max(scores, -1))
    weights = jnp.where(visible[None, None], jnp.exp(scores - new_peak[..., None]), 0.0)
    total = jnp.sum(weights, -1)
    accum = jnp.einsum(
        "jgtc,cjd->jgtd", weights.astype(jnp.bfloat16), values, preferred_element_type=jnp.float32
    )
    peak, total, accum = (new_peak, total, accum)
    mixed = (
        (accum / total[..., None])
        .transpose(2, 0, 1, 3)
        .reshape(tokens, q_width)
        .astype(jnp.bfloat16)
    )
    partial_value = jnp.dot(mixed, w_out, preferred_element_type=jnp.float32)
    ends = (
        jnp.sum(
            (seg_row[None, :] <= jnp.arange(1, responses + 1, dtype=jnp.int32)[:, None]).astype(
                jnp.int32
            ),
            1,
        )
        - 1
    )
    at_end = (ends == block) & (phase_now == phases - 1)
    summed = lax.psum(partial_value.astype(jnp.bfloat16), "mp").astype(jnp.float32)
    updated = (state_wide + summed).astype(jnp.bfloat16)
    moved = passed_along(updated, "section", 1)
    last_row = updated[tokens - 1].astype(jnp.float32)
    squares = jnp.sum(last_row * last_row)
    product = jnp.sum(last_row * final_gain * reward_head)
    sums_sq, dots = lax.psum(
        (jnp.where(at_end, squares, 0.0), jnp.where(at_end, product, 0.0)), ("section", "dp")
    )
    rewards = dots * lax.rsqrt(sums_sq / width + EPS)
    pair_loss = jnp.where(
        ranks[:, None] < ranks[None, :], jax.nn.softplus(rewards[None, :] - rewards[:, None]), 0.0
    )
    return (moved[None], rewards, pair_loss)


def solution(mesh):
    placed = (
        P("section", "dp", None),
        P("section", None),
        P("section", None, "mp"),
        P("section", "mp", "dp"),
        P(),
        P(),
        P("section", None),
        P(),
    )
    return jax.shard_map(
        shards,
        mesh=mesh,
        in_specs=placed,
        out_specs=(P("section", "dp", None), P(), P()),
        check_vma=False,
    )
```

profile of v0, /device:TPU:24, one launch (start us, length us, event | category | flops | bytes accessed | tf_op | source)
XLA Modules:
  0.0 862.3 jit_solution(7415746184136145379)
XLA Ops:
  7.2 0.7 all-gather.3.cloned.1.call-update
  8.7 2.9 fusion.16
  11.7 16.4 %all_gather.6 = bf16[512,512]{1,0:T(8,128)(2,1)S(1)} all-gather(bf16[128,512]{1,0:T(8,128)(2,1)S(1)} %fusion.16), channel_id=1, replica_groups=mesh['section'=2,'dp'=4,'mp'=4] {'dp'}, dimensions={0}, use_global_device_ids=true | all-gather | bytes 655360 | tf_op jit(solution)/shard_map/all_gather | solution.py:48
  28.2 0.7 fusion.48
  28.9 0.7 copy.22
  29.7 0.6 fusion.44
  30.4 0.7 or_and_fusion
  31.2 537.7 %all-gather.3.cloned.1.call-done = bf16[1,1,8388608]{2,1,0:T(2,128)(2,1)} async-done(((bf16[1,1,2097152]{2,1,0:T(2,128)(2,1)}), bf16[1,1,8388608]{2,1,0:T(2,128)(2,1)}) %all-gather.3.cloned.1.call-update) | async-done | bytes 16777232 | tf_op jit(solution)/shard_map/all_gather | solution.py:40
  568.9 183.8 %slice_reduce_fusion = (bf16[4194304]{0:T(1024)(128)(2,1)}, bf16[4194304]{0:T(1024)(128)(2,1)}) fusion(bf16[1,1,8388608]{2,1,0:T(2,128)(2,1)} %all-gather.3.cloned.1.call-done), kind=kLoop, calls=%fused_computation | loop fusion | bytes 33554432 | tf_op jit(solution)/shard_map/slice | solution.py:42
  752.8 13.3 %slice.40 = bf16[1024,4096]{1,0:T(8,128)(2,1)} reshape(bf16[4194304]{0:T(1024)(128)(2,1)} %get-tuple-element.3) | data formatting | bytes 16777216 | tf_op jit(solution)/shard_map/slice | solution.py:42
  766.1 13.3 %slice.37 = bf16[4096,1024]{1,0:T(8,128)(2,1)} reshape(bf16[4194304]{0:T(1024)(128)(2,1)} %get-tuple-element.4) | data formatting | bytes 16777216 | tf_op jit(solution)/shard_map/slice | solution.py:41
  779.4 4.7 convolution_convert_fusion.1
  785.3 0.7 fusion.15
  785.9 1.7 copy-done
  787.6 2.3 convolution_convert_fusion
  790.1 37.3 %all-reduce.3.cloned.1.call-done = bf16[128,4096]{1,0:T(8,128)(2,1)} async-done(((bf16[128,4096]{1,0:T(8,128)(2,1)}), bf16[128,4096]{1,0:T(8,128)(2,1)}) %all-reduce.3.cloned.1.call-update) | async-done | bytes 1048592 | tf_op jit(solution)/shard_map/psum | solution.py:88
  827.4 1.5 fusion.8
  828.9 3.4 collective-permute-start
  832.4 0.6 multiply_reduce_fusion
  833.0 1.3 broadcast_select_fusion
  834.3 17.1 %all-reduce = (f32[2]{0:T(128)S(1)}, f32[2]{0:T(128)S(1)}) all-reduce(f32[2]{0:T(128)S(1)} %get-tuple-element.12, f32[2]{0:T(128)S(1)} %get-tuple-element.11), channel_id=1, replica_groups=mesh['section'=2,'dp'=4,'mp'=4] {'section','dp'}, use_global_device_ids=true, to_apply=%region_8.9 | all-reduce | flops 4 | bytes 32 | tf_op jit(solution)/shard_map/psum | solution.py:94
  851.4 0.7 compare_select_fusion.1
  852.0 2.5 collective-permute-done
  854.5 1.0 copy.34
  (33 shorter events, 2.6 us)
Async XLA Ops:
  7.2 1.2 copy-start.1
  7.2 1.5 copy-start.7
  7.2 561.7 %all-gather.3.cloned.1.call-start = ((), (), s32[]{:S(2)}) async-start(), calls=%async_computation.1 | async-start | bytes 41943040 | tf_op jit(solution)/shard_map/all_gather | solution.py:40
  7.9 819.5 %all-reduce.3.cloned.1.call-start = ((), (), s32[]{:S(2)}) async-start(), calls=%async_computation | async-start | bytes 2097152 | tf_op jit(solution)/shard_map/psum | solution.py:88
  28.1 1.6 copy-start.6
  784.2 3.4 copy-start
  789.9 42.5 %copy-start.2 = (f32[4096]{0:T(1024)S(1)}, f32[4096]{0:T(1024)}, u32[]{:S(2)}) copy-start(f32[4096]{0:T(1024)} %param.13) | copy-start | bytes 49156
  789.9 42.5 %copy-start.3 = (f32[4096]{0:T(1024)S(1)}, f32[4096]{0:T(1024)}, u32[]{:S(2)}) copy-start(f32[4096]{0:T(1024)} %param.12) | copy-start | bytes 49156
  789.9 61.5 %copy-start.4 = (s32[2]{0:T(128)S(1)}, s32[2]{0:T(128)}, u32[]{:S(2)}) copy-start(s32[2]{0:T(128)} %param.15) | copy-start | bytes 28
  828.9 25.6 %collective-permute-start = (bf16[128,4096]{1,0:T(8,128)(2,1)S(1)}, bf16[128,4096]{1,0:T(8,128)(2,1)S(1)}, u32[]{:S(2)}, u32[]{:S(2)}) collective-permute-start(bf16[128,4096]{1,0:T(8,128)(2,1)S(1)} %fusion.8), channel_id=1, source_target_pairs={{0,16},{1,17},{2,18},{3,19},{4,20},{5,21},{6,22},{7,23},{8,24},{9,... | collective-permute-start | bytes 3145736 | tf_op jit(solution)/shard_map/ppermute | solution.py:17
  851.4 4.1 copy-start.5
Sparse Core Ops, SparseCore 0:
  9.6 559.2 all-gather.2
  790.0 37.3 all-reduce.2
where the time goes:
time: 865 us; the launch traced here: 862 us
  waiting for transfers between devices  578 us (67%)
  local copies, waits for them, and re-layouts  215 us (25%)
  blocking collectives  33.5 us (4%)
  between operations  14.2 us (2%)
  matrix products  11 us (1%)
    all_gather x1, waiting for transfers between devices, shards(): flat = lax.all_gather(attn_flat[0, 0], 'dp', axis=0, tiled=True)  538 us
    slice x2, local copies, waits for them, and re-layouts, shards(): w_out = flat[width * q_width:2 * width * q_width].reshape(q_width, width)  197 us
    psum x1, waiting for transfers between devices, shards(): lax.psum(partial_value.astype(jnp.bfloat16), 'mp').astype(jnp.float32)  37.3 us
  transfers between devices with their start and end apart: 3, of which 3 were waited for; matrix products, arithmetic and copies ran while one was open for 1% of the time, Pallas kernels for 0%

commit v1 on v0

--- a/solution.py
+++ b/solution.py
@@ -1,6 +1,10 @@
+import functools
+
 import jax
 import jax.numpy as jnp
 from jax import lax
+from jax.experimental import pallas as pl
+from jax.experimental.pallas import tpu as pltpu
 from jax.sharding import PartitionSpec as P
 
 HD = 128
@@ -17,7 +21,7 @@
     return lax.ppermute(block, axis, route)
 
 
-def shards(hidden, norm_gain, kv_weight, attn_flat, final_gain, reward_head, segment_ids, ranks):
+def gathered_shards(hidden, norm_gain, kv_weight, attn_flat, final_gain, reward_head, segment_ids, ranks):
     state = hidden[0]
     tokens = state.shape[0]
     width = state.shape[1]
@@ -101,6 +105,602 @@
     return (moved[None], rewards, pair_loss)
 
 
+BF = jnp.bfloat16
+F32 = jnp.float32
+HIDE = -1e30
+
+
+def copy_to(src, dst, send, recv, **where):
+    return pltpu.make_async_remote_copy(
+        src_ref=src,
+        dst_ref=dst,
+        send_sem=send,
+        recv_sem=recv,
+        device_id=where,
+        device_id_type=pl.DeviceIdType.MESH,
+    )
+
+
+def relay_kernel(
+    phases,
+    h_ref,
+    gain_ref,
+    kvw_hbm,
+    flat_hbm,
+    hide_ref,
+    pick_ref,
+    fg_ref,
+    rh_ref,
+    out_ref,
+    stat_ref,
+    kvw,
+    flat,
+    wq,
+    wo,
+    nrm,
+    xq,
+    kvs,
+    kvr,
+    qs,
+    qo,
+    qr,
+    mx,
+    mr,
+    osend,
+    oown,
+    orecv,
+    ysend,
+    yown,
+    yrecv,
+    zsend,
+    zrecv,
+    ts,
+    tr,
+    us,
+    fin,
+    st,
+    res,
+    sres,
+    load_sem,
+    nz_s,
+    nz_r,
+    nm_s,
+    nm_r,
+    kv_s,
+    kv_r,
+    q_s,
+    q_r,
+    m_s,
+    m_r,
+    o_s,
+    o_r,
+    y_s,
+    y_r,
+    z_s,
+    z_r,
+    t_s,
+    t_r,
+    u_s,
+    u_r,
+    f_s,
+    f_r,
+    st_s,
+    st_r,
+    sr_s,
+    sr_r,
+):
+    s = lax.axis_index("section")
+    d = lax.axis_index("dp")
+    m = lax.axis_index("mp")
+    y = m // 2
+    c = m % 2
+    across = (m + 2) % 4
+    beside = m + 1 - 2 * c
+    load_kv = pltpu.make_async_copy(kvw_hbm.at[0], kvw, load_sem.at[0])
+    load_flat = pltpu.make_async_copy(flat_hbm, flat, load_sem.at[1])
+    load_kv.start()
+    load_flat.start()
+
+    barrier = pltpu.get_barrier_semaphore()
+    place = d * 4 + m
+    for k in range(1, 16):
+        t = (place + k) % 16
+        pl.semaphore_signal(
+            barrier,
+            inc=1,
+            device_id={"dp": t // 4, "mp": t % 4},
+            device_id_type=pl.DeviceIdType.MESH,
+        )
+    for k in range(1, phases):
+        pl.semaphore_signal(
+            barrier,
+            inc=1,
+            device_id={"section": (s + k) % phases},
+            device_id_type=pl.DeviceIdType.MESH,
+        )
+    h = h_ref[...].astype(F32)
+    scale = lax.rsqrt(jnp.mean(h * h, -1, keepdims=True) + EPS)
+    nrm[...] = (h * scale * gain_ref[...]).astype(BF)
+    pl.semaphore_wait(barrier, 15 + phases - 1)
+
+    quarter = pl.ds(pl.multiple_of(m * 32, 32), 32)
+    far_quarter = pl.ds(pl.multiple_of(across * 32, 32), 32)
+
+    def hop_z(t):
+        return copy_to(
+            nrm.at[quarter, t * 2048 : (t + 1) * 2048],
+            xq.at[d, quarter],
+            nz_s.at[t],
+            nz_r.at[d],
+            dp=t,
+        )
+
+    def arrive_z(b):
+        return copy_to(xq.at[b, quarter], xq.at[b, quarter], nz_s.at[0], nz_r.at[b], dp=b)
+
+    def spread(b, k):
+        rows = far_quarter if k == 2 else quarter
+        return copy_to(
+            xq.at[b, rows],
+            xq.at[b, rows],
+            nm_s.at[b, k],
+            nm_r.at[b, k],
+            mp=across if k == 0 else beside,
+        )
+
+    def kv_hop(t):
+        return copy_to(kvs.at[t], kvr.at[d], kv_s.at[t], kv_r.at[d], dp=t)
+
+    def kv_arrive(b):
+        return copy_to(kvr.at[b], kvr.at[b], kv_s.at[0], kv_r.at[b], dp=b)
+
+    for t in range(2):
+
+        @pl.when(d != t)
+        def _():
+            hop_z(t).start()
+
+        @pl.when(d == t)
+        def _():
+            xq[t] = nrm[:, t * 2048 : (t + 1) * 2048]
+
+    load_kv.wait()
+    for t in range(2):
+        kvs[t] = jnp.dot(
+            nrm[...], kvw[:, t * 256 : (t + 1) * 256], preferred_element_type=F32
+        ).astype(BF)
+
+        @pl.when(d != t)
+        def _():
+            kv_hop(t).start()
+
+        @pl.when(d == t)
+        def _():
+            kvr[t] = kvs[t]
+
+    load_flat.wait()
+
+    def q_copy(b):
+        return copy_to(qs.at[b], qr.at[b], q_s.at[b], q_r.at[b], dp=1 - d)
+
+    def m_copy(b):
+        return copy_to(mx.at[b], mr.at[b], m_s.at[b], m_r.at[b], dp=d + 2)
+
+    def m_arrive(b):
+        return copy_to(mr.at[b], mr.at[b], m_s.at[b], m_r.at[b], dp=d - 2)
+
+    @pl.when(d < 2)
+    def _():
+        for b in range(4):
+
+            @pl.loop(0, 8)
+            def _(i):
+                i = i + b * 8
+                part = flat[0, :, pl.ds(pl.multiple_of(i * 65536, 65536), 65536)].astype(F32)
+                wq[pl.ds(pl.multiple_of(i * 64, 64), 64), :] = part.reshape(64, 1024).astype(BF)
+
+            @pl.when(d != b)
+            def _():
+                arrive_z(b).wait_recv()
+                spread(b, 0).start()
+                spread(b, 1).start()
+
+        def forward(b):
+            @pl.when(d != b)
+            def _():
+                spread(b, 0).wait_recv()
+                spread(b, 2).start()
+
+        def project(b):
+            @pl.when(d != b)
+            def _():
+                spread(b, 1).wait_recv()
+                spread(b, 2).wait_recv()
+
+            mine = pl.ds(pl.multiple_of(d * 512, 512), 512)
+            other = pl.ds(pl.multiple_of((1 - d) * 512, 512), 512)
+            qs[b] = jnp.dot(xq[b], wq[:, other], preferred_element_type=F32).astype(BF)
+            q_copy(b).start()
+            qo[b] = jnp.dot(xq[b], wq[:, mine], preferred_element_type=F32)
+
+        def attend(b):
+            q_copy(b).wait_recv()
+
+            @pl.when(d != b)
+            def _():
+                kv_arrive(b).wait_recv()
+
+            q = (qo[b] + qr[b].astype(F32)).astype(BF)
+            q = jnp.concatenate([q[:, j * HD : (j + 1) * HD] for j in range(4)], 0)
+            scores = []
+            for j in range(b + 1):
+                score = (
+                    lax.dot_general(
+                        q, kvr[j, :, :HD], (((1,), (1,)), ((), ())), preferred_element_type=F32
+                    )
+                    * HD ** (-0.5)
+                )
+                if j < b:
+                    score = score + hide_ref[b * 4 + j : b * 4 + j + 1, :]
+                else:
+                    row = lax.broadcasted_iota(jnp.int32, score.shape, 0) % 128
+                    col = lax.broadcasted_iota(jnp.int32, score.shape, 1)
+                    score = jnp.where(col <= row, score, HIDE)
+                scores.append(score)
+            peak = functools.reduce(jnp.maximum, [jnp.max(x, -1, keepdims=True) for x in scores])
+            total = jnp.zeros_like(peak)
+            mixed = jnp.zeros((512, HD), F32)
+            for j in range(b + 1):
+                weight = jnp.exp(scores[j] - peak)
+                total = total + jnp.sum(weight, -1, keepdims=True)
+                mixed = mixed + jnp.dot(
+                    weight.astype(BF), kvr[j, :, HD:], preferred_element_type=F32
+                )
+            mixed = (mixed / total).astype(BF)
+            for j in range(4):
+                mx[b, :, j * HD : (j + 1) * HD] = mixed[j * 128 : (j + 1) * 128]
+            m_copy(b).start()
+
+        forward(0)
+        for b in range(5):
+            if b < 3:
+                forward(b + 1)
+            if b < 4:
+                project(b)
+            if b >= 1:
+                attend(b - 1)
+
+    def o_copy(b):
+        return copy_to(osend.at[b], orecv.at[b], o_s.at[b], o_r.at[b], mp=beside)
+
+    def y_copy(b):
+        return copy_to(ysend.at[b], yrecv.at[b], y_s.at[b], y_r.at[b], mp=across)
+
+    def z_copy(b):
+        return copy_to(zsend.at[b], zrecv.at[b], z_s.at[b], z_r.at[b], dp=5 - d)
+
+    def t_copy(b):
+        return copy_to(ts.at[b], tr, t_s.at[b], t_r, dp=b)
+
+    def t_arrive():
+        return copy_to(tr, tr, t_s.at[0], t_r, dp=2)
+
+    mine_out = pl.ds(pl.multiple_of((2 * c + y) * 1024, 1024), 1024)
+
+    def finish(total):
+        fresh = (h_ref[:, mine_out].astype(F32) + total).astype(BF)
+        us[...] = fresh
+
+    @pl.when(d >= 2)
+    def _():
+        @pl.loop(0, 32)
+        def _(i):
+            part = flat[0, :, pl.ds(pl.multiple_of(i * 65536, 65536), 65536)].astype(F32)
+            wo[pl.ds(pl.multiple_of(i * 16, 16), 16), :] = part.reshape(16, 4096).astype(BF)
+
+        def first(b):
+            m_arrive(b).wait_recv()
+            mine = pl.ds(pl.multiple_of(c * 2048, 2048), 2048)
+            other = pl.ds(pl.multiple_of((1 - c) * 2048, 2048), 2048)
+            osend[b] = jnp.dot(mr[b], wo[:, other], preferred_element_type=F32).astype(BF)
+            o_copy(b).start()
+            oown[b] = jnp.dot(mr[b], wo[:, mine], preferred_element_type=F32)
+
+        def second(b):
+            o_copy(b).wait_recv()
+            mine = pl.ds(pl.multiple_of(y * 1024, 1024), 1024)
+            other = pl.ds(pl.multiple_of((1 - y) * 1024, 1024), 1024)
+            ysend[b] = (oown[b, :, other] + orecv[b, :, other].astype(F32)).astype(BF)
+            y_copy(b).start()
+            yown[b] = oown[b, :, mine] + orecv[b, :, mine].astype(F32)
+
+        def third(b):
+            y_copy(b).wait_recv()
+            keeper = 3 if b == 3 else 2
+
+            @pl.when(d != keeper)
+            def _():
+                zsend[b] = (yown[b] + yrecv[b].astype(F32)).astype(BF)
+                z_copy(b).start()
+
+            @pl.when(d == keeper)
+            def _():
+                yown[b] = yown[b] + yrecv[b].astype(F32)
+
+        def fourth(b):
+            keeper = 3 if b == 3 else 2
+
+            @pl.when(d == keeper)
+            def _():
+                z_copy(b).wait_recv()
+                total = yown[b] + zrecv[b].astype(F32)
+                if b < 2:
+                    ts[b] = total.astype(BF)
+                    t_copy(b).start()
+                else:
+                    finish(total)
+
+        for step in range(7):
+            for part, stage in enumerate((first, second, third, fourth)):
+                if 0 <= step - part < 4:
+                    stage(step - part)
+
+    @pl.when(d < 2)
+    def _():
+        t_arrive().wait_recv()
+        finish(tr[...].astype(F32))
+
+    def u_copy():
+        return copy_to(us, fin.at[m], u_s, u_r, section=s + 1)
+
+    def u_arrive():
+        return copy_to(fin.at[m], fin.at[m], u_s, u_r, section=s - 1)
+
+    def f_copy(k):
+        which = across if k == 2 else m
+        return copy_to(
+            fin.at[which], fin.at[which], f_s.at[k], f_r.at[k], mp=across if k == 0 else beside
+        )
+
+    @pl.when(s < phases - 1)
+    def _():
+        u_copy().start()
+
+    row = us[120:128, :].astype(F32)[7:8, :]
+    squares = jnp.sum(row * row, keepdims=True)
+    product = jnp.sum(row * fg_ref[:, mine_out] * rh_ref[:, mine_out], keepdims=True)
+    half = lax.broadcasted_iota(jnp.int32, (8, 128), 0) < 4
+    st[place] = jnp.where(half, squares, product)
+
+    def st_copy(k):
+        t = (place + k) % 16
+        return pltpu.make_async_remote_copy(
+            src_ref=st.at[place],
+            dst_ref=st.at[place],
+            send_sem=st_s.at[k - 1],
+            recv_sem=st_r.at[k - 1],
+            device_id={"dp": t // 4, "mp": t % 4},
+            device_id_type=pl.DeviceIdType.MESH,
+        )
+
+    def st_arrive(k):
+        t = (place + 16 - k) % 16
+        return pltpu.make_async_remote_copy(
+            src_ref=st.at[t],
+            dst_ref=st.at[t],
+            send_sem=st_s.at[k - 1],
+            recv_sem=st_r.at[k - 1],
+            device_id={"dp": t // 4, "mp": t % 4},
+            device_id_type=pl.DeviceIdType.MESH,
+        )
+
+    def sr_copy(k):
+        return copy_to(res, sres, sr_s.at[k - 1], sr_r, section=(s + k) % phases)
+
+    @pl.when(s == phases - 1)
+    def _():
+        for k in range(1, 16):
+            st_copy(k).start()
+
+    @pl.when(s == 0)
+    def _():
+        out_ref[...] = jnp.zeros_like(out_ref)
+
+    @pl.when(s > 0)
+    def _():
+        u_arrive().wait_recv()
+        f_copy(0).start()
+        f_copy(1).start()
+        f_copy(0).wait_recv()
+        f_copy(2).start()
+
+    @pl.when(s == phases - 1)
+    def _():
+        for k in range(1, 16):
+            st_arrive(k).wait_recv()
+        for r in range(pick_ref.shape[0]):
+            at_end = jnp.zeros((8, 128), F32)
+            for b in range(4):
+                block = st[4 * b] + st[4 * b + 1] + st[4 * b + 2] + st[4 * b + 3]
+                at_end = at_end + jnp.where(pick_ref[r, b] > 0, block, 0.0)
+            res[r] = at_end
+        for k in range(1, phases):
+            sr_copy(k).start()
+        stat_ref[...] = res[...]
+
+    @pl.when(s > 0)
+    def _():
+        f_copy(1).wait_recv()
+        f_copy(2).wait_recv()
+        for k in range(4):
+            spot = 2 * (k % 2) + k // 2
+            out_ref[:, spot * 1024 : (spot + 1) * 1024] = fin[k]
+        for k in range(3):
+            f_copy(k).wait_send()
+
+    @pl.when(s < phases - 1)
+    def _():
+        sr_copy(1).wait_recv()
+        stat_ref[...] = sres[...]
+        u_copy().wait_send()
+
+    @pl.when(s == phases - 1)
+    def _():
+        for k in range(1, 16):
+            st_copy(k).wait_send()
+        for k in range(1, phases):
+            sr_copy(k).wait_send()
+
+    for t in range(2):
+
+        @pl.when(d != t)
+        def _():
+            hop_z(t).wait_send()
+            kv_hop(t).wait_send()
+
+    @pl.when(d < 2)
+    def _():
+        for b in range(4):
+
+            @pl.when(d != b)
+            def _():
+                for k in range(3):
+                    spread(b, k).wait_send()
+
+            q_copy(b).wait_send()
+            m_copy(b).wait_send()
+
+    @pl.when(d >= 2)
+    def _():
+        for b in range(4):
+            o_copy(b).wait_send()
+            y_copy(b).wait_send()
+            keeper = 3 if b == 3 else 2
+
+            @pl.when(d != keeper)
+            def _():
+                z_copy(b).wait_send()
+
+            if b < 2:
+
+                @pl.when(d == keeper)
+                def _():
+                    t_copy(b).wait_send()
+
+
+def kept_shards(hidden, norm_gain, kv_weight, attn_flat, final_gain, reward_head, segment_ids, ranks):
+    width = hidden.shape[2]
+    seg = segment_ids[0]
+    phases = lax.axis_size("section")
+    responses = ranks.shape[0]
+    seen = (seg[None, :] == 0) | (seg[None, :] == seg[:, None])
+    hide = jnp.broadcast_to(jnp.where(seen, 0.0, HIDE).reshape(16, 1), (16, 128)).astype(F32)
+    level = jnp.arange(1, responses + 1, dtype=jnp.int32)
+    ends = jnp.sum((seg[None, :] <= level[:, None]).astype(jnp.int32), 1) - 1
+    pick = (ends[:, None] == jnp.arange(4, dtype=jnp.int32)[None, :]).astype(F32)
+    pick = jnp.broadcast_to(pick[:, :, None, None], (responses, 4, 8, 128))
+    vmem = pl.BlockSpec(memory_space=pltpu.VMEM)
+    anywhere = pl.BlockSpec(memory_space=pl.ANY)
+    dma = pltpu.SemaphoreType.DMA
+    V = pltpu.VMEM
+    moved, stats = pl.pallas_call(
+        functools.partial(relay_kernel, phases),
+        out_shape=(
+            jax.ShapeDtypeStruct((128, 4096), BF),
+            jax.ShapeDtypeStruct((responses, 8, 128), F32),
+        ),
+        in_specs=[vmem, vmem, anywhere, anywhere, vmem, vmem, vmem, vmem],
+        out_specs=(vmem, vmem),
+        scratch_shapes=[
+            V((4096, 512), BF),
+            V((1, 1, 2097152), BF),
+            V((2048, 1024), BF),
+            V((512, 4096), BF),
+            V((128, 4096), BF),
+            V((4, 128, 2048), BF),
+            V((2, 128, 256), BF),
+            V((4, 128, 256), BF),
+            V((4, 128, 512), BF),
+            V((4, 128, 512), F32),
+            V((4, 128, 512), BF),
+            V((4, 128, 512), BF),
+            V((4, 128, 512), BF),
+            V((4, 128, 2048), BF),
+            V((4, 128, 2048), F32),
+            V((4, 128, 2048), BF),
+            V((4, 128, 1024), BF),
+            V((4, 128, 1024), F32),
+            V((4, 128, 1024), BF),
+            V((4, 128, 1024), BF),
+            V((4, 128, 1024), BF),
+            V((2, 128, 1024), BF),
+            V((128, 1024), BF),
+            V((128, 1024), BF),
+            V((4, 128, 1024), BF),
+            V((16, 8, 128), F32),
+            V((responses, 8, 128), F32),
+            V((responses, 8, 128), F32),
+            dma((2,)),
+            dma((2,)),
+            dma((4,)),
+            dma((4, 3)),
+            dma((4, 3)),
+            dma((2,)),
+            dma((4,)),
+            dma((4,)),
+            dma((4,)),
+            dma((4,)),
+            dma((4,)),
+            dma((4,)),
+            dma((4,)),
+            dma((4,)),
+            dma((4,)),
+            dma((4,)),
+            dma((4,)),
+            dma((2,)),
+            dma(()),
+            dma(()),
+            dma(()),
+            dma((3,)),
+            dma((3,)),
+            dma((15,)),
+            dma((15,)),
+            dma((max(phases - 1, 1),)),
+            dma(()),
+        ],
+        compiler_params=pltpu.CompilerParams(
+            collective_id=0, has_side_effects=True, vmem_limit_bytes=60 << 20
+        ),
+    )(
+        hidden[0],
+        norm_gain,
+        kv_weight,
+        attn_flat,
+        hide,
+        pick,
+        final_gain[None],
+        reward_head[None],
+    )
+    rewards = stats[:, 4, 0] * lax.rsqrt(stats[:, 0, 0] / width + EPS)
+    pair_loss = jnp.where(
+        ranks[:, None] < ranks[None, :], jax.nn.softplus(rewards[None, :] - rewards[:, None]), 0.0
+    )
+    return (moved[None], rewards, pair_loss)
+
+
+def shards(hidden, norm_gain, kv_weight, attn_flat, final_gain, reward_head, segment_ids, ranks):
+    blocks = lax.axis_size("dp")
+    lanes = lax.axis_size("mp")
+    kv_local = kv_weight.shape[2] // (2 * HD)
+    kept = (
+        (blocks, lanes, kv_local) == (4, 4, 2)
+        and hidden.shape[1:] == (128, 4096)
+        and attn_flat.shape == (1, 1, 2097152)
+    )
+    args = (hidden, norm_gain, kv_weight, attn_flat, final_gain, reward_head, segment_ids, ranks)
+    return (kept_shards if kept else gathered_shards)(*args)
+
+
 def solution(mesh):
     placed = (
         P("section", "dp", None),

time: 865 us -> 94.6 us (0.11)
  waiting for transfers between devices: 578 us -> 0 us
  local copies, waits for them, and re-layouts: 215 us -> 3.74 us
  Pallas kernels: 0 us -> 84.6 us
  blocking collectives: 33.5 us -> 0 us
  between operations: 14.2 us -> 0.66 us
  matrix products: 11 us -> 0 us
    all_gather x1 -> x0, waiting for transfers between devices: 538 us -> none  [shards(): flat = lax.all_gather(attn_flat[0, 0], 'dp', axis=0, tiled=True)]
    slice x4 -> x0, local copies, waits for them, and re-layouts: 211 us -> none  [the longest x2 197 us: shards(): w_out = flat[width * q_width:2 * width * q_width].reshape(q_width, width)]
    pallas_call x0 -> x1, Pallas kernels: none -> 84.6 us  [kept_shards(): pl.pallas_call(functools.partial(relay_kernel, phases), out_shape=(jax.Sh...]
    psum x1 -> x0, waiting for transfers between devices: 37.3 us -> none  [shards(): lax.psum(partial_value.astype(jnp.bfloat16), 'mp').astype(jnp.float32)]
    psum x1 -> x0, blocking collectives: 17.1 us -> none  [shards(): lax.psum((jnp.where(at_end, squares, 0.0), jnp.where(at_end, product, 0.0...]
    all_gather x1 -> x0, blocking collectives: 16.4 us -> none  [shards(): piece = lax.all_gather(keyval, 'dp', axis=0, tiled=True)]
    dot_general x5 -> x0, matrix products: 11 us -> none  [the longest x1 4.68 us: shards(): jnp.dot(normed, w_query, preferred_element_type=jnp.float32)]
  transfers between devices with their start and end apart: 3 -> 0, of which waited for: 3 -> 0; matrix products, arithmetic and copies ran while one was open for 1% -> 0% of each run, Pallas kernels for 0% -> 0%
where the time goes in v1:
time: 94.6 us; the launch traced here: 92.9 us
  Pallas kernels  84.6 us (89%)
  other arithmetic  3.91 us (4%)
  local copies, waits for them, and re-layouts  3.74 us (4%)
    pallas_call x1, Pallas kernels, kept_shards(): pl.pallas_call(functools.partial(relay_kernel, phases), out_shape=(jax.Sh...  84.6 us
    unnamed x5, local copies, waits for them, and re-layouts  2.29 us

profile of v1, /device:TPU:24, one launch (start us, length us, event | category | flops | bytes accessed | tf_op | source)
XLA Modules:
  0.0 92.9 jit_solution(7027759569698264762)
XLA Ops:
  0.6 0.0 copy-start.1
  0.7 0.8 fusion.4
  1.5 0.1 compare_convert_fusion
  1.6 0.7 broadcast_in_dim.40.pick_ref
  2.3 0.7 compare_bitcast_fusion
  2.9 0.8 or_select_fusion
  3.7 0.1 select_n.20
  3.8 0.7 broadcast_in_dim.22.hide_ref
  4.5 84.6 %shard_map.103 = (bf16[128,4096]{1,0:T(8,128)(2,1)}, f32[2,8,128]{2,1,0:T(8,128)}) custom-call(bf16[128,4096]{1,0:T(8,128)(2,1)} %bitcast.7, f32[1,4096]{1,0:T(1,128)} %gain_ref.1, bf16[1,4096,512]{2,1,0:T(8,128)(2,1)} %kvw_hbm.1, bf16[1,1,2097152]{2,1,0:T(2,128)(2,1)} %flat_hbm.1, f32[16,128]{1,0:T(8,128)} %broadcast_in_dim.22.hide_ref, ...), custom_call_target="tpu_custom_call" | custom-call | tf_op jit(solution)/shard_map/pallas_call | solution.py:606
  89.1 0.9 multiply_reduce_fusion
  89.9 0.0 copy-done.1
  89.9 0.0 copy-start
  90.0 0.7 compare_select_fusion.1
  90.6 2.3 %copy.12 = bf16[1,128,4096]{2,1,0:T(8,128)(2,1)} copy(bf16[1,128,4096]{2,1,0:T(8,128)(2,1)} %bitcast.8) | data formatting | bytes 2097152
  92.9 0.0 copy-done
  (2 shorter events, 0.0 us)
Async XLA Ops:
  0.6 89.3 %copy-start.1 = (s32[2]{0:T(128)S(1)}, s32[2]{0:T(128)}, u32[]{:S(2)}) copy-start(s32[2]{0:T(128)} %param.15) | copy-start | bytes 28
  89.9 2.9 %copy-start = (f32[2]{0:T(128)}, f32[2]{0:T(128)S(1)}, u32[]{:S(2)}) copy-start(f32[2]{0:T(128)S(1)} %multiply_reduce_fusion) | copy-start | bytes 28

commit v2 on v1

--- a/solution.py
+++ b/solution.py
@@ -127,8 +127,7 @@
     gain_ref,
     kvw_hbm,
     flat_hbm,
-    hide_ref,
-    pick_ref,
+    seg_ref,
     fg_ref,
     rh_ref,
     out_ref,
@@ -289,6 +288,15 @@
     def m_arrive(b):
         return copy_to(mr.at[b], mr.at[b], m_s.at[b], m_r.at[b], dp=d - 2)
 
+    def piece(g, stage):
+        if g % 2:
+            stage(g)
+        else:
+
+            @pl.when(s < phases - 1)
+            def _():
+                stage(g)
+
     @pl.when(d < 2)
     def _():
         for b in range(4):
@@ -323,14 +331,17 @@
             q_copy(b).start()
             qo[b] = jnp.dot(xq[b], wq[:, mine], preferred_element_type=F32)
 
-        def attend(b):
+        def ready(b):
             q_copy(b).wait_recv()
 
             @pl.when(d != b)
             def _():
                 kv_arrive(b).wait_recv()
 
-            q = (qo[b] + qr[b].astype(F32)).astype(BF)
+        def attend(g):
+            b, half = g // 2, g % 2
+            rows = slice(half * 64, half * 64 + 64)
+            q = (qo[b, rows] + qr[b, rows].astype(F32)).astype(BF)
             q = jnp.concatenate([q[:, j * HD : (j + 1) * HD] for j in range(4)], 0)
             scores = []
             for j in range(b + 1):
@@ -341,15 +352,16 @@
                     * HD ** (-0.5)
                 )
                 if j < b:
-                    score = score + hide_ref[b * 4 + j : b * 4 + j + 1, :]
+                    seen = (seg_ref[0, j] == 0) | (seg_ref[0, j] == seg_ref[0, b])
+                    score = score + jnp.where(seen, 0.0, HIDE)
                 else:
-                    row = lax.broadcasted_iota(jnp.int32, score.shape, 0) % 128
+                    row = lax.broadcasted_iota(jnp.int32, score.shape, 0) % 64 + half * 64
                     col = lax.broadcasted_iota(jnp.int32, score.shape, 1)
                     score = jnp.where(col <= row, score, HIDE)
                 scores.append(score)
             peak = functools.reduce(jnp.maximum, [jnp.max(x, -1, keepdims=True) for x in scores])
             total = jnp.zeros_like(peak)
-            mixed = jnp.zeros((512, HD), F32)
+            mixed = jnp.zeros((256, HD), F32)
             for j in range(b + 1):
                 weight = jnp.exp(scores[j] - peak)
                 total = total + jnp.sum(weight, -1, keepdims=True)
@@ -358,8 +370,8 @@
                 )
             mixed = (mixed / total).astype(BF)
             for j in range(4):
-                mx[b, :, j * HD : (j + 1) * HD] = mixed[j * 128 : (j + 1) * 128]
-            m_copy(b).start()
+                mx[g, :, j * HD : (j + 1) * HD] = mixed[j * 64 : (j + 1) * 64]
+            m_copy(g).start()
 
         forward(0)
         for b in range(5):
@@ -368,7 +380,9 @@
             if b < 4:
                 project(b)
             if b >= 1:
-                attend(b - 1)
+                ready(b - 1)
+                piece(2 * b - 2, attend)
+                piece(2 * b - 1, attend)
 
     def o_copy(b):
         return copy_to(osend.at[b], orecv.at[b], o_s.at[b], o_r.at[b], mp=beside)
@@ -380,16 +394,36 @@
         return copy_to(zsend.at[b], zrecv.at[b], z_s.at[b], z_r.at[b], dp=5 - d)
 
     def t_copy(b):
-        return copy_to(ts.at[b], tr, t_s.at[b], t_r, dp=b)
-
-    def t_arrive():
-        return copy_to(tr, tr, t_s.at[0], t_r, dp=2)
+        return copy_to(ts.at[b], tr.at[b % 2], t_s.at[b], t_r.at[b % 2], dp=b // 2)
+
+    def t_arrive(p):
+        return copy_to(tr.at[p], tr.at[p], t_s.at[0], t_r.at[p], dp=2)
 
     mine_out = pl.ds(pl.multiple_of((2 * c + y) * 1024, 1024), 1024)
 
-    def finish(total):
-        fresh = (h_ref[:, mine_out].astype(F32) + total).astype(BF)
-        us[...] = fresh
+    def u_copy(p):
+        return copy_to(us.at[p], fin.at[p, m], u_s.at[p], u_r.at[p], section=s + 1)
+
+    def u_arrive(p):
+        return copy_to(fin.at[p, m], fin.at[p, m], u_s.at[p], u_r.at[p], section=s - 1)
+
+    def f_copy(p, k):
+        which = across if k == 2 else m
+        return copy_to(
+            fin.at[p, which],
+            fin.at[p, which],
+            f_s.at[p, k],
+            f_r.at[p, k],
+            mp=across if k == 0 else beside,
+        )
+
+    def finish(p, total):
+        old = h_ref[p * 64 : p * 64 + 64, mine_out].astype(F32)
+        us[p] = (old + total).astype(BF)
+
+        @pl.when(s < phases - 1)
+        def _():
+            u_copy(p).start()
 
     @pl.when(d >= 2)
     def _():
@@ -416,7 +450,7 @@
 
         def third(b):
             y_copy(b).wait_recv()
-            keeper = 3 if b == 3 else 2
+            keeper = 3 if b >= 6 else 2
 
             @pl.when(d != keeper)
             def _():
@@ -428,45 +462,33 @@
                 yown[b] = yown[b] + yrecv[b].astype(F32)
 
         def fourth(b):
-            keeper = 3 if b == 3 else 2
+            keeper = 3 if b >= 6 else 2
 
             @pl.when(d == keeper)
             def _():
                 z_copy(b).wait_recv()
                 total = yown[b] + zrecv[b].astype(F32)
-                if b < 2:
+                if b < 4:
                     ts[b] = total.astype(BF)
                     t_copy(b).start()
                 else:
-                    finish(total)
-
-        for step in range(7):
+                    finish(b % 2, total)
+
+        for step in range(11):
             for part, stage in enumerate((first, second, third, fourth)):
-                if 0 <= step - part < 4:
-                    stage(step - part)
+                if 0 <= step - part < 8:
+                    piece(step - part, stage)
 
     @pl.when(d < 2)
     def _():
-        t_arrive().wait_recv()
-        finish(tr[...].astype(F32))
-
-    def u_copy():
-        return copy_to(us, fin.at[m], u_s, u_r, section=s + 1)
-
-    def u_arrive():
-        return copy_to(fin.at[m], fin.at[m], u_s, u_r, section=s - 1)
-
-    def f_copy(k):
-        which = across if k == 2 else m
-        return copy_to(
-            fin.at[which], fin.at[which], f_s.at[k], f_r.at[k], mp=across if k == 0 else beside
-        )
-
-    @pl.when(s < phases - 1)
-    def _():
-        u_copy().start()
-
-    row = us[120:128, :].astype(F32)[7:8, :]
+        def close(p):
+            t_arrive(p).wait_recv()
+            finish(p, tr[p].astype(F32))
+
+        piece(0, close)
+        piece(1, close)
+
+    row = us[1, 48:64, :].astype(F32)[15:16, :]
     squares = jnp.sum(row * row, keepdims=True)
     product = jnp.sum(row * fg_ref[:, mine_out] * rh_ref[:, mine_out], keepdims=True)
     half = lax.broadcasted_iota(jnp.int32, (8, 128), 0) < 4
@@ -508,21 +530,26 @@
 
     @pl.when(s > 0)
     def _():
-        u_arrive().wait_recv()
-        f_copy(0).start()
-        f_copy(1).start()
-        f_copy(0).wait_recv()
-        f_copy(2).start()
+        for p in range(2):
+            u_arrive(p).wait_recv()
+            f_copy(p, 0).start()
+            f_copy(p, 1).start()
+        for p in range(2):
+            f_copy(p, 0).wait_recv()
+            f_copy(p, 2).start()
 
     @pl.when(s == phases - 1)
     def _():
         for k in range(1, 16):
             st_arrive(k).wait_recv()
-        for r in range(pick_ref.shape[0]):
+        for r in range(res.shape[0]):
+            end = -1
+            for b in range(4):
+                end = end + jnp.where(seg_ref[0, b] <= r + 1, 1, 0)
             at_end = jnp.zeros((8, 128), F32)
             for b in range(4):
                 block = st[4 * b] + st[4 * b + 1] + st[4 * b + 2] + st[4 * b + 3]
-                at_end = at_end + jnp.where(pick_ref[r, b] > 0, block, 0.0)
+                at_end = at_end + block * jnp.where(end == b, 1.0, 0.0)
             res[r] = at_end
         for k in range(1, phases):
             sr_copy(k).start()
@@ -530,19 +557,21 @@
 
     @pl.when(s > 0)
     def _():
-        f_copy(1).wait_recv()
-        f_copy(2).wait_recv()
-        for k in range(4):
-            spot = 2 * (k % 2) + k // 2
-            out_ref[:, spot * 1024 : (spot + 1) * 1024] = fin[k]
-        for k in range(3):
-            f_copy(k).wait_send()
+        for p in range(2):
+            f_copy(p, 1).wait_recv()
+            f_copy(p, 2).wait_recv()
+            for k in range(4):
+                out_ref[2 * (k % 2) + k // 2, p * 64 : p * 64 + 64] = fin[p, k]
+        for p in range(2):
+            for k in range(3):
+                f_copy(p, k).wait_send()
 
     @pl.when(s < phases - 1)
     def _():
         sr_copy(1).wait_recv()
         stat_ref[...] = sres[...]
-        u_copy().wait_send()
+        for p in range(2):
+            u_copy(p).wait_send()
 
     @pl.when(s == phases - 1)
     def _():
@@ -568,37 +597,34 @@
                     spread(b, k).wait_send()
 
             q_copy(b).wait_send()
-            m_copy(b).wait_send()
+        for g in range(8):
+            piece(g, lambda g: m_copy(g).wait_send())
 
     @pl.when(d >= 2)
     def _():
-        for b in range(4):
-            o_copy(b).wait_send()
-            y_copy(b).wait_send()
-            keeper = 3 if b == 3 else 2
+        def sent(g):
+            o_copy(g).wait_send()
+            y_copy(g).wait_send()
+            keeper = 3 if g >= 6 else 2
 
             @pl.when(d != keeper)
             def _():
-                z_copy(b).wait_send()
-
-            if b < 2:
+                z_copy(g).wait_send()
+
+            if g < 4:
 
                 @pl.when(d == keeper)
                 def _():
-                    t_copy(b).wait_send()
+                    t_copy(g).wait_send()
+
+        for g in range(8):
+            piece(g, sent)
 
 
 def kept_shards(hidden, norm_gain, kv_weight, attn_flat, final_gain, reward_head, segment_ids, ranks):
     width = hidden.shape[2]
-    seg = segment_ids[0]
     phases = lax.axis_size("section")
     responses = ranks.shape[0]
-    seen = (seg[None, :] == 0) | (seg[None, :] == seg[:, None])
-    hide = jnp.broadcast_to(jnp.where(seen, 0.0, HIDE).reshape(16, 1), (16, 128)).astype(F32)
-    level = jnp.arange(1, responses + 1, dtype=jnp.int32)
-    ends = jnp.sum((seg[None, :] <= level[:, None]).astype(jnp.int32), 1) - 1
-    pick = (ends[:, None] == jnp.arange(4, dtype=jnp.int32)[None, :]).astype(F32)
-    pick = jnp.broadcast_to(pick[:, :, None, None], (responses, 4, 8, 128))
     vmem = pl.BlockSpec(memory_space=pltpu.VMEM)
     anywhere = pl.BlockSpec(memory_space=pl.ANY)
     dma = pltpu.SemaphoreType.DMA
@@ -606,10 +632,18 @@
     moved, stats = pl.pallas_call(
         functools.partial(relay_kernel, phases),
         out_shape=(
-            jax.ShapeDtypeStruct((128, 4096), BF),
+            jax.ShapeDtypeStruct((4, 128, 1024), BF),
             jax.ShapeDtypeStruct((responses, 8, 128), F32),
         ),
-        in_specs=[vmem, vmem, anywhere, anywhere, vmem, vmem, vmem, vmem],
+        in_specs=[
+            vmem,
+            vmem,
+            anywhere,
+            anywhere,
+            pl.BlockSpec(memory_space=pltpu.SMEM),
+            vmem,
+            vmem,
+        ],
         out_specs=(vmem, vmem),
         scratch_shapes=[
             V((4096, 512), BF),
@@ -623,20 +657,20 @@
             V((4, 128, 512), BF),
             V((4, 128, 512), F32),
             V((4, 128, 512), BF),
-            V((4, 128, 512), BF),
-            V((4, 128, 512), BF),
-            V((4, 128, 2048), BF),
-            V((4, 128, 2048), F32),
-            V((4, 128, 2048), BF),
-            V((4, 128, 1024), BF),
-            V((4, 128, 1024), F32),
-            V((4, 128, 1024), BF),
-            V((4, 128, 1024), BF),
-            V((4, 128, 1024), BF),
-            V((2, 128, 1024), BF),
-            V((128, 1024), BF),
-            V((128, 1024), BF),
-            V((4, 128, 1024), BF),
+            V((8, 64, 512), BF),
+            V((8, 64, 512), BF),
+            V((8, 64, 2048), BF),
+            V((8, 64, 2048), F32),
+            V((8, 64, 2048), BF),
+            V((8, 64, 1024), BF),
+            V((8, 64, 1024), F32),
+            V((8, 64, 1024), BF),
+            V((8, 64, 1024), BF),
+            V((8, 64, 1024), BF),
+            V((4, 64, 1024), BF),
+            V((2, 64, 1024), BF),
+            V((2, 64, 1024), BF),
+            V((2, 4, 64, 1024), BF),
             V((16, 8, 128), F32),
             V((responses, 8, 128), F32),
             V((responses, 8, 128), F32),
@@ -649,20 +683,20 @@
             dma((4,)),
             dma((4,)),
             dma((4,)),
-            dma((4,)),
-            dma((4,)),
-            dma((4,)),
-            dma((4,)),
-            dma((4,)),
-            dma((4,)),
-            dma((4,)),
+            dma((8,)),
+            dma((8,)),
+            dma((8,)),
+            dma((8,)),
+            dma((8,)),
+            dma((8,)),
+            dma((8,)),
+            dma((8,)),
             dma((4,)),
             dma((2,)),
-            dma(()),
-            dma(()),
-            dma(()),
-            dma((3,)),
-            dma((3,)),
+            dma((2,)),
+            dma((2,)),
+            dma((2, 3)),
+            dma((2, 3)),
             dma((15,)),
             dma((15,)),
             dma((max(phases - 1, 1),)),
@@ -676,8 +710,7 @@
         norm_gain,
         kv_weight,
         attn_flat,
-        hide,
-        pick,
+        segment_ids,
         final_gain[None],
         reward_head[None],
     )
@@ -685,7 +718,8 @@
     pair_loss = jnp.where(
         ranks[:, None] < ranks[None, :], jax.nn.softplus(rewards[None, :] - rewards[:, None]), 0.0
     )
-    return (moved[None], rewards, pair_loss)
+    moved = moved.transpose(1, 0, 2).reshape(1, 128, width)
+    return (moved, rewards, pair_loss)
 
 
 def shards(hidden, norm_gain, kv_weight, attn_flat, final_gain, reward_head, segment_ids, ranks):

time: 94.6 us -> 91.3 us (0.965); the launches traced: 92.9 us -> 91 us
  other arithmetic: 3.91 us -> 1.53 us
  Pallas kernels: 84.6 us -> 85.9 us
    transpose x0 -> x1, local copies, waits for them, and re-layouts: none -> 1.61 us  [kept_shards(): moved = moved.transpose(1, 0, 2).reshape(1, 128, width)]
    broadcast_in_dim x2 -> x0, local copies, waits for them, and re-layouts: 1.36 us -> none  [the longest x1 0.69 us: kept_shards(): pick = jnp.broadcast_to(pick[:, :, None, None], (responses, 4, 8, 128))]
    pallas_call x1, Pallas kernels: 84.6 us -> 85.9 us  [kept_shards(): pl.pallas_call(functools.partial(relay_kernel, phases), out_shape=(jax.Sh...]
    unnamed x5, local copies, waits for them, and re-layouts: 2.29 us -> 1.32 us
where the time goes in v2:
time: 91.3 us; the launch traced here: 91 us
  Pallas kernels  85.9 us (94%)
  local copies, waits for them, and re-layouts  2.93 us (3%)
  other arithmetic  1.53 us (2%)
    pallas_call x1, Pallas kernels, kept_shards(): pl.pallas_call(functools.partial(relay_kernel, phases), out_shape=(jax.Sh...  85.9 us

profile of v2, /device:TPU:24, one launch (start us, length us, event | category | flops | bytes accessed | tf_op | source)
XLA Modules:
  0.0 91.0 jit_solution(17008636734920583392)
XLA Ops:
  0.6 0.0 copy-start.1
  0.6 85.9 %shard_map.103 = (bf16[4,128,1024]{2,1,0:T(8,128)(2,1)}, f32[2,8,128]{2,1,0:T(8,128)}) custom-call(bf16[128,4096]{1,0:T(8,128)(2,1)} %bitcast.7, f32[1,4096]{1,0:T(1,128)} %gain_ref.1, bf16[1,4096,512]{2,1,0:T(8,128)(2,1)} %kvw_hbm.1, bf16[1,1,2097152]{2,1,0:T(2,128)(2,1)} %flat_hbm.1, s32[1,4]{1,0:T(1,128)} %seg_ref.1, f32[1,4096]{1,0:T(1,128)} %bitcast.8, ...), custom_call_target="tpu_custom_call" | custom-call | tf_op jit(solution)/shard_map/pallas_call | solution.py:632
  86.5 0.9 multiply_reduce_fusion
  87.4 0.0 copy-done.1
  87.4 0.0 copy-start
  87.4 0.7 compare_select_fusion.1
  88.1 1.6 %copy.11 = bf16[128,4,1024]{0,2,1:T(8,128)(2,1)S(1)} copy(bf16[128,4,1024]{2,0,1:T(8,128)(2,1)} %bitcast.6) | data formatting | bytes 2097152 | tf_op jit(solution)/shard_map/transpose | solution.py:721
  89.7 1.3 %copy.12 = bf16[1,128,4096]{2,1,0:T(8,128)(2,1)} copy(bf16[1,128,4096]{1,2,0:T(8,128)(2,1)S(1)} %bitcast.5) | data formatting | bytes 2097152
  91.0 0.0 copy-done
Async XLA Ops:
  0.6 86.8 %copy-start.1 = (s32[2]{0:T(128)S(1)}, s32[2]{0:T(128)}, u32[]{:S(2)}) copy-start(s32[2]{0:T(128)} %param.15) | copy-start | bytes 28
  87.4 3.6 %copy-start = (f32[2]{0:T(128)}, f32[2]{0:T(128)S(1)}, u32[]{:S(2)}) copy-start(f32[2]{0:T(128)S(1)} %multiply_reduce_fusion) | copy-start | bytes 28

commit v3 on v2

--- a/solution.py
+++ b/solution.py
@@ -299,14 +299,14 @@
 
     @pl.when(d < 2)
     def _():
-        for b in range(4):
-
+        def reshape(b):
             @pl.loop(0, 8)
             def _(i):
                 i = i + b * 8
                 part = flat[0, :, pl.ds(pl.multiple_of(i * 65536, 65536), 65536)].astype(F32)
                 wq[pl.ds(pl.multiple_of(i * 64, 64), 64), :] = part.reshape(64, 1024).astype(BF)
 
+        def receive(b):
             @pl.when(d != b)
             def _():
                 arrive_z(b).wait_recv()
@@ -373,12 +373,21 @@
                 mx[g, :, j * HD : (j + 1) * HD] = mixed[j * 64 : (j + 1) * 64]
             m_copy(g).start()
 
+        reshape(0)
+        receive(0)
+        reshape(1)
+        receive(1)
+        reshape(2)
         forward(0)
+        reshape(3)
+        forward(1)
         for b in range(5):
-            if b < 3:
-                forward(b + 1)
+            if b < 2:
+                receive(b + 2)
             if b < 4:
                 project(b)
+            if b < 2:
+                forward(b + 2)
             if b >= 1:
                 ready(b - 1)
                 piece(2 * b - 2, attend)
@@ -474,8 +483,8 @@
                 else:
                     finish(b % 2, total)
 
-        for step in range(11):
-            for part, stage in enumerate((first, second, third, fourth)):
+        for step in range(10):
+            for part, stage in ((0, first), (1, third), (2, fourth), (0, second)):
                 if 0 <= step - part < 8:
                     piece(step - part, stage)
 

time: 91.3 us -> 95.7 us (1.048)
  Pallas kernels: 85.9 us -> 90.4 us
    pallas_call x1, Pallas kernels: 85.9 us -> 90.4 us  [kept_shards(): pl.pallas_call(functools.partial(relay_kernel, phases), out_shape=(jax.Sh...]
where the time goes in v3:
time: 95.7 us; the launch traced here: 95.5 us
  Pallas kernels  90.4 us (94%)
  local copies, waits for them, and re-layouts  2.93 us (3%)
  other arithmetic  1.53 us (2%)
    pallas_call x1, Pallas kernels, kept_shards(): pl.pallas_call(functools.partial(relay_kernel, phases), out_shape=(jax.Sh...  90.4 us

profile of v3, /device:TPU:24, one launch (start us, length us, event | category | flops | bytes accessed | tf_op | source)
XLA Modules:
  0.0 95.5 jit_solution(4399522228568843800)
XLA Ops:
  0.6 0.0 copy-start.1
  0.6 90.4 %shard_map.103 = (bf16[4,128,1024]{2,1,0:T(8,128)(2,1)}, f32[2,8,128]{2,1,0:T(8,128)}) custom-call(bf16[128,4096]{1,0:T(8,128)(2,1)} %bitcast.7, f32[1,4096]{1,0:T(1,128)} %gain_ref.1, bf16[1,4096,512]{2,1,0:T(8,128)(2,1)} %kvw_hbm.1, bf16[1,1,2097152]{2,1,0:T(2,128)(2,1)} %flat_hbm.1, s32[1,4]{1,0:T(1,128)} %seg_ref.1, f32[1,4096]{1,0:T(1,128)} %bitcast.8, ...), custom_call_target="tpu_custom_call" | custom-call | tf_op jit(solution)/shard_map/pallas_call | solution.py:641
  91.0 0.9 multiply_reduce_fusion
  91.9 0.0 copy-done.1
  91.9 0.0 copy-start
  91.9 0.7 compare_select_fusion.1
  92.5 1.6 %copy.11 = bf16[128,4,1024]{0,2,1:T(8,128)(2,1)S(1)} copy(bf16[128,4,1024]{2,0,1:T(8,128)(2,1)} %bitcast.6) | data formatting | bytes 2097152 | tf_op jit(solution)/shard_map/transpose | solution.py:730
  94.2 1.3 %copy.12 = bf16[1,128,4096]{2,1,0:T(8,128)(2,1)} copy(bf16[1,128,4096]{1,2,0:T(8,128)(2,1)S(1)} %bitcast.5) | data formatting | bytes 2097152
  95.5 0.0 copy-done
Async XLA Ops:
  0.6 91.2 %copy-start.1 = (s32[2]{0:T(128)S(1)}, s32[2]{0:T(128)}, u32[]{:S(2)}) copy-start(s32[2]{0:T(128)} %param.15) | copy-start | bytes 28
  91.9 3.6 %copy-start = (f32[2]{0:T(128)}, f32[2]{0:T(128)S(1)}, u32[]{:S(2)}) copy-start(f32[2]{0:T(128)S(1)} %multiply_reduce_fusion) | copy-start | bytes 28

commit v4 on v2

--- a/solution.py
+++ b/solution.py
@@ -299,14 +299,14 @@
 
     @pl.when(d < 2)
     def _():
-        for b in range(4):
-
+        def reshape(b):
             @pl.loop(0, 8)
             def _(i):
                 i = i + b * 8
                 part = flat[0, :, pl.ds(pl.multiple_of(i * 65536, 65536), 65536)].astype(F32)
                 wq[pl.ds(pl.multiple_of(i * 64, 64), 64), :] = part.reshape(64, 1024).astype(BF)
 
+        def receive(b):
             @pl.when(d != b)
             def _():
                 arrive_z(b).wait_recv()
@@ -373,12 +373,19 @@
                 mx[g, :, j * HD : (j + 1) * HD] = mixed[j * 64 : (j + 1) * 64]
             m_copy(g).start()
 
+        for b in range(3):
+            reshape(b)
+            receive(b)
+        reshape(3)
         forward(0)
+        forward(1)
         for b in range(5):
-            if b < 3:
-                forward(b + 1)
             if b < 4:
                 project(b)
+            if b == 0:
+                receive(3)
+            if b < 2:
+                forward(b + 2)
             if b >= 1:
                 ready(b - 1)
                 piece(2 * b - 2, attend)
@@ -475,7 +482,7 @@
                     finish(b % 2, total)
 
         for step in range(11):
-            for part, stage in enumerate((first, second, third, fourth)):
+            for part, stage in ((0, first), (1, second), (2, third), (3, fourth)):
                 if 0 <= step - part < 8:
                     piece(step - part, stage)
 
@@ -523,10 +530,6 @@
     def _():
         for k in range(1, 16):
             st_copy(k).start()
-
-    @pl.when(s == 0)
-    def _():
-        out_ref[...] = jnp.zeros_like(out_ref)
 
     @pl.when(s > 0)
     def _():
@@ -561,7 +564,8 @@
             f_copy(p, 1).wait_recv()
             f_copy(p, 2).wait_recv()
             for k in range(4):
-                out_ref[2 * (k % 2) + k // 2, p * 64 : p * 64 + 64] = fin[p, k]
+                spot = (2 * (k % 2) + k // 2) * 1024
+                out_ref[p * 64 : p * 64 + 64, spot : spot + 1024] = fin[p, k]
         for p in range(2):
             for k in range(3):
                 f_copy(p, k).wait_send()
@@ -632,7 +636,7 @@
     moved, stats = pl.pallas_call(
         functools.partial(relay_kernel, phases),
         out_shape=(
-            jax.ShapeDtypeStruct((4, 128, 1024), BF),
+            jax.ShapeDtypeStruct((128, 4096), BF),
             jax.ShapeDtypeStruct((responses, 8, 128), F32),
         ),
         in_specs=[
@@ -718,8 +722,8 @@
     pair_loss = jnp.where(
         ranks[:, None] < ranks[None, :], jax.nn.softplus(rewards[None, :] - rewards[:, None]), 0.0
     )
-    moved = moved.transpose(1, 0, 2).reshape(1, 128, width)
-    return (moved, rewards, pair_loss)
+    moved = jnp.where(lax.axis_index("section") > 0, moved, jnp.zeros_like(moved))
+    return (moved[None], rewards, pair_loss)
 
 
 def shards(hidden, norm_gain, kv_weight, attn_flat, final_gain, reward_head, segment_ids, ranks):

time: 91.3 us -> 88.6 us (0.970)
  local copies, waits for them, and re-layouts: 2.93 us -> 0.01 us
  other arithmetic: 1.53 us -> 2.57 us
    transpose x1 -> x0, local copies, waits for them, and re-layouts: 1.61 us -> none  [kept_shards(): moved = moved.transpose(1, 0, 2).reshape(1, 128, width)]
    unnamed x5 -> x4, local copies, waits for them, and re-layouts: 1.32 us -> 0.01 us
    broadcast_in_dim x0 -> x1, other arithmetic: none -> 1.04 us  [kept_shards(): return (moved[None], rewards, pair_loss)]
where the time goes in v4:
time: 88.6 us; the launch traced here: 88.4 us
  Pallas kernels  85.2 us (96%)
  other arithmetic  2.57 us (3%)
    pallas_call x1, Pallas kernels, kept_shards(): pl.pallas_call(functools.partial(relay_kernel, phases), out_shape=(jax.Sh...  85.2 us

profile of v4, /device:TPU:24, one launch (start us, length us, event | category | flops | bytes accessed | tf_op | source)
XLA Modules:
  0.0 88.4 jit_solution(9834592331158175892)
XLA Ops:
  0.6 0.0 copy-start.1
  0.6 85.2 %shard_map.103 = (bf16[128,4096]{1,0:T(8,128)(2,1)}, f32[2,8,128]{2,1,0:T(8,128)}) custom-call(bf16[128,4096]{1,0:T(8,128)(2,1)} %bitcast.5, f32[1,4096]{1,0:T(1,128)} %gain_ref.1, bf16[1,4096,512]{2,1,0:T(8,128)(2,1)} %kvw_hbm.1, bf16[1,1,2097152]{2,1,0:T(2,128)(2,1)} %flat_hbm.1, s32[1,4]{1,0:T(1,128)} %seg_ref.1, f32[1,4096]{1,0:T(1,128)} %bitcast.6, ...), custom_call_target="tpu_custom_call" | custom-call | tf_op jit(solution)/shard_map/pallas_call | solution.py:636
  85.8 0.9 multiply_reduce_fusion
  86.7 0.0 copy-done.1
  86.7 0.0 copy-start
  86.7 0.7 compare_select_fusion.1
  87.4 1.0 %select_bitcast_fusion = bf16[1,128,4096]{2,1,0:T(8,128)(2,1)} fusion(bf16[128,4096]{1,0:T(8,128)(2,1)} %get-tuple-element.5, pred[]{:T(512)S(6)} %gt.3), kind=kLoop, calls=%fused_computation | loop fusion | flops 524288 | bytes 2097153 | tf_op jit(solution)/shard_map/broadcast_in_dim | solution.py:726
  88.4 0.0 copy-done
Async XLA Ops:
  0.6 86.1 %copy-start.1 = (s32[2]{0:T(128)S(1)}, s32[2]{0:T(128)}, u32[]{:S(2)}) copy-start(s32[2]{0:T(128)} %param.15) | copy-start | bytes 28
  86.7 1.7 %copy-start = (f32[2]{0:T(128)}, f32[2]{0:T(128)S(1)}, u32[]{:S(2)}) copy-start(f32[2]{0:T(128)S(1)} %multiply_reduce_fusion) | copy-start | bytes 28
